TPU v7x, 32 devices: a whole 2x2x4 slice. The times are simulated.
32 devices in a mesh: obj: 16 (over z, x, core), ep: 2 (over y).
Axes of the slice: x: 2, y: 2, z: 4, core: 2. Of those that a mesh axis runs over, the one named last changes fastest.
Arguments:
- light_curves: float32 [2048, 256], P('obj', 'ep'), may hold values from -40 to 40
- valid: int32 [2048, 256], P('obj', 'ep'), may hold values 0 or 1
- pixel: int32 [2048], P('obj'), may hold values from 0 to 63, never falling along the last dimension, each value on 1 to 64 neighbouring positions
- inv_sigma: float32 [2048], P('obj'), may hold values from 0.5 to 4
- modes_init: float32 [256, 16], P('ep'), may hold values from -6 to 6
- epoch_jitter: float32 [256], replicated, may hold values from 0 to 0.9
- freq_index: int32 [2048], replicated, may hold values from 4 to 511
Outputs:
- residual: float32 [2048, 256], P('obj', 'ep')
- power: float32 [2048, 2048], P(('obj', 'ep'))
Inputs may be any that keep to these rules, and one draw needn't show every extreme that they name: Pixels never decrease along the objects; each pixel holds 1 to 64 objects, and some pixel exactly 64.
All inputs are finite; a program needn't handle non-finite values. No bound on the sum of `valid` on one device may be relied on, other than what follows from the above.
Results may differ from a plain program's by a relative error of at most 0.0052.
Values may be sent and summed in bfloat16 or wider, within the bound.
A program may use at most 64 MiB of HBM per device.

v0:
```python
import functools
import math

import jax
import jax.numpy as jnp
from jax import lax
from jax.experimental import pallas as pl
from jax.experimental.pallas import tpu as pltpu
from jax.sharding import PartitionSpec as P

ITERS = 2


HUBER = 1.345
DAMP = 2.0
RIDGE = 0.05
HIGHEST = lax.Precision.HIGHEST
LANES = 128
SUB = 8
F32 = jnp.float32
STRIP = 32
MESH = pl.DeviceIdType.MESH


def first_of(row):
    return SUB * (row // SUB)


def packed_outer(vectors):
    order = vectors.shape[0]
    return jnp.concatenate(
        [vectors[i : i + 1] * vectors[first_of(i) :] for i in range(order)], axis=0
    )


def damped_solve(packed, order):
    level = lax.broadcasted_iota(jnp.int32, (order, packed.shape[1]), 0)
    rows = []
    at = 0
    for i in range(order):
        low = first_of(i)
        rows.append(packed[at : at + order - low] + DAMP * (level[low:] == i).astype(F32))
        at += order - low
    remain = packed[at : at + order]
    inverse, forward = [], []
    for k in range(order):
        low = first_of(k)
        row = rows[k]
        inverse.append(1.0 / row[k - low : k - low + 1])
        scaled = row * inverse[k]
        for j in range(k + 1, order):
            begin = first_of(j)
            rows[j] = rows[j] - scaled[j - low : j - low + 1] * row[begin - low :]
        forward.append(remain[k : k + 1])
        part = remain[low:] - scaled * forward[k]
        remain = part if low == 0 else jnp.concatenate([remain[:low], part], axis=0)
    solved = jnp.zeros((order, packed.shape[1]), F32)
    for k in reversed(range(order)):
        low = first_of(k)
        known = jnp.sum(rows[k] * solved[low:], axis=0, keepdims=True)
        value = (forward[k] - known) * inverse[k]
        solved = jnp.where(level == k, value, solved)
    return solved


def spread_out(values, rows, cols):
    down, right = rows - values.shape[0], cols - values.shape[1]
    return jnp.pad(values, ((0, down), (0, right)))


def as_column(row):
    return jnp.broadcast_to(row, (LANES, row.shape[1])).T


def detrend_kernel(
    obj_n, ep_n, order, near, lc_ref, valid_ref, pixel_ref, sigma_ref, modes_ref,
    jitter_ref, freq_ref, resid_ref, power_ref, basis_s, times_s,
    coef_s, modes_s, pix_send, pix_recv, ep_send, ep_recv, gram_send, gram_recv,
    mode_send, mode_recv, half_send, half_recv,
    pix_sem, ep_sem, gram_sem, mode_sem, half_sem,
):
    me_o, me_e = lax.axis_index("obj"), lax.axis_index("ep")
    rows, cols = lc_ref.shape
    blocks = cols // SUB
    share = rows // ep_n

    def device(do, de):
        return {
            "obj": lax.rem(me_o + do, obj_n),
            "ep": lax.rem(me_e + de, ep_n),
        }

    peers = list(near)
    peers += [(do, 0) for do in range(1, obj_n) if (do, 0) not in near]
    barrier = pltpu.get_barrier_semaphore()
    for do, de in peers:
        pl.semaphore_signal(barrier, inc=1, device_id=device(do, de), device_id_type=MESH)
    pl.semaphore_wait(barrier, len(peers))

    def sends_to(do):
        return None if do == 0 else me_o < obj_n - 1 if do == 1 else me_o > 0

    def hears_from(do):
        return None if do == 0 else me_o > 0 if do == 1 else me_o < obj_n - 1

    def guarded(condition, action):
        if condition is None:
            action()
        else:
            pl.when(condition)(action)

    for k, (do, de) in enumerate(near):
        if do != 0:
            @pl.when(jnp.logical_not(hears_from(do)))
            def _():
                pix_recv[:, k] = jnp.zeros(pix_recv.shape[:1] + pix_recv.shape[2:], F32)

    mask = valid_ref[...].astype(F32)
    sigma = as_column(sigma_ref[...])[:, :1]
    epochs = jitter_ref.shape[1]
    times_s[...] = as_column(
        lax.broadcasted_iota(jnp.int32, (1, epochs), 1).astype(F32) + jitter_ref[...]
    )
    width = basis_s.shape[3]

    def fill_basis(block):
        begin = pl.multiple_of(block * width, width)
        freqs = (freq_ref[:, pl.ds(begin, width)] + 1).astype(F32) / (4.0 * epochs)

        def strip(step, carry):
            at = pl.ds(pl.multiple_of(step * STRIP, STRIP), STRIP)
            times = jnp.concatenate([times_s[at, :]] * (width // LANES), axis=1)
            for kind, values in enumerate(basis_of(times * freqs)):
                basis_s[block, kind, at, :] = values.astype(jnp.bfloat16)
            return carry

        lax.fori_loop(0, epochs // STRIP, strip, 0)

    pixels = lax.broadcasted_iota(jnp.int32, (rows, pix_send.shape[2]), 1)
    member = (as_column(pixel_ref[...].astype(F32))[:, :1] == pixels.astype(F32)).astype(F32)
    counts = jnp.sum(member * jnp.sum(mask, axis=1, keepdims=True), axis=0, keepdims=True)

    def residual():
        return lc_ref[...] - lax.dot_general(
            coef_s[...], modes_s[...], (((0,), (0,)), ((), ())),
            precision=HIGHEST, preferred_element_type=F32,
        )

    def robust(resid, phase, block=None):
        scaled = resid * sigma
        squares = jnp.sum(mask * scaled * scaled, axis=1, keepdims=True)
        sums = jnp.sum(member * squares, axis=0, keepdims=True)
        part = spread_out(jnp.concatenate([sums, counts], axis=0), SUB, sums.shape[1])
        pix_send[phase] = part
        copies = []
        for k, (do, de) in enumerate(near):
            copies.append(pltpu.make_async_remote_copy(
                src_ref=pix_send.at[phase], dst_ref=pix_recv.at[phase, k],
                send_sem=pix_sem.at[0, phase, k], recv_sem=pix_sem.at[1, phase, k],
                device_id=device(do, de), device_id_type=MESH,
            ))
            guarded(sends_to(do), copies[k].start)
        if block is not None:
            fill_basis(block)
        for k, (do, de) in enumerate(near):
            guarded(sends_to(do), copies[k].wait_send)
            guarded(hears_from(do), copies[k].wait_recv)
        totals = part
        for k in range(len(near)):
            totals = totals + pix_recv[phase, k]
        spread = jnp.sqrt(totals[0:1] / jnp.maximum(totals[1:2], 1.0) + 1e-06)
        object_spread = jnp.sum(member * spread, axis=1, keepdims=True)
        zscore = scaled / object_spread
        huber = HUBER / jnp.maximum(jnp.abs(zscore), HUBER)
        return mask * huber * (sigma * sigma)

    coef_s[...] = jnp.zeros_like(coef_s)
    modes_s[...] = modes_ref[...]

    def iteration(it, carry):
        light = lc_ref[...]
        weight = robust(residual(), 2 * it, 4 * it)
        modes_t = modes_s[...]
        last = (((1,), (1,)), ((), ()))
        gram = lax.dot_general(
            packed_outer(modes_t), weight, last, precision=HIGHEST, preferred_element_type=F32
        )
        target = lax.dot_general(
            modes_t, weight * light, last, precision=HIGHEST, preferred_element_type=F32
        )
        packed = jnp.concatenate([gram, target], axis=0)
        ep_send[it] = packed
        copies = []
        for k in range(1, ep_n):
            copies.append(pltpu.make_async_remote_copy(
                src_ref=ep_send.at[it], dst_ref=ep_recv.at[it, k - 1],
                send_sem=ep_sem.at[0, it, k - 1], recv_sem=ep_sem.at[1, it, k - 1],
                device_id=device(0, k), device_id_type=MESH,
            ))
            copies[-1].start()
        for k in range(1, ep_n):
            copies[k - 1].wait()
            packed = packed + ep_recv[it, k - 1]
        coef_t = damped_solve(packed, order)
        coef_s[...] = coef_t

        weight = robust(residual(), 2 * it + 1, 4 * it + 1)
        gram = jnp.dot(
            packed_outer(coef_t), weight, precision=HIGHEST, preferred_element_type=F32
        )
        target = jnp.dot(
            coef_t, weight * light, precision=HIGHEST, preferred_element_type=F32
        )
        packed = jnp.concatenate([gram, target], axis=0)
        depth = packed.shape[0]
        wide = gram_send.shape[3]
        turned = spread_out(packed, wide, cols).T
        gram_send[it] = turned.reshape(blocks, SUB, wide)
        copies = []
        for k in range(1, obj_n):
            there = lax.rem(me_o + k, obj_n)
            copies.append(pltpu.make_async_remote_copy(
                src_ref=gram_send.at[it, lax.rem(there, blocks)],
                dst_ref=gram_recv.at[it, k - 1],
                send_sem=gram_sem.at[0, it, k - 1], recv_sem=gram_sem.at[1, it, k - 1],
                device_id=device(k, 0), device_id_type=MESH,
            ))
            copies[-1].start()
        fill_basis(4 * it + 2)
        total = gram_send[it, lax.rem(me_o, blocks)]
        for k in range(1, obj_n):
            copies[k - 1].wait()
            total = total + gram_recv[it, k - 1]
        packed = spread_out(total, LANES, wide).T[:depth]
        solved = damped_solve(packed, order)
        mine = spread_out(solved, LANES, LANES).T[:SUB]
        mode_send[it] = mine
        mode_recv[it, me_o] = mine
        copies = []
        for k in range(1, obj_n):
            copies.append(pltpu.make_async_remote_copy(
                src_ref=mode_send.at[it], dst_ref=mode_recv.at[it, me_o],
                send_sem=mode_sem.at[0, it, k - 1], recv_sem=mode_sem.at[1, it, k - 1],
                device_id=device(k, 0), device_id_type=MESH,
            ))
            copies[-1].start()
        fill_basis(4 * it + 3)
        for copy in copies:
            copy.wait()
        modes_s[...] = mode_recv[it, :blocks].reshape(cols, LANES).T[:order]
        return carry

    lax.fori_loop(0, ITERS, iteration, 0)
    resid = residual()
    resid_ref[...] = resid
    weight = robust(resid, 2 * ITERS)
    half_send[0] = (weight * resid).astype(jnp.bfloat16)
    half_send[1] = weight.astype(jnp.bfloat16)
    copies = []
    for k in range(1, ep_n):
        there = lax.rem(me_e + k, ep_n)
        copies.append(pltpu.make_async_remote_copy(
            src_ref=half_send.at[:, pl.ds(pl.multiple_of(there * share, share), share), :],
            dst_ref=half_recv.at[me_e],
            send_sem=half_sem.at[0, k - 1], recv_sem=half_sem.at[1, k - 1],
            device_id=device(0, k), device_id_type=MESH,
        ))
        copies[-1].start()
    half_recv[me_e] = half_send[:, pl.ds(pl.multiple_of(me_e * share, share), share), :]
    for copy in copies:
        copy.wait()
    received = [half_recv[e] for e in range(ep_n)]
    values = jnp.concatenate([half[0] for half in received], axis=1)
    weights = jnp.concatenate([half[1] for half in received], axis=1)
    both = jnp.concatenate([weights, values], axis=0)
    total = jnp.sum(weights.astype(F32), axis=1, keepdims=True)
    level = jnp.sum(values.astype(F32), axis=1, keepdims=True)

    def spectrum(block, carry):
        at = pl.ds(pl.multiple_of(block * width, width), width)
        power_ref[:, at] = powers(
            jnp.dot(both, basis_s[block, 0], preferred_element_type=F32),
            jnp.dot(both, basis_s[block, 1], preferred_element_type=F32),
            jnp.dot(weights, basis_s[block, 2], preferred_element_type=F32),
            jnp.dot(weights, basis_s[block, 3], preferred_element_type=F32),
            total,
            level,
        )
        return carry

    lax.fori_loop(0, basis_s.shape[0], spectrum, 0)


SIN_TERMS = [(-1.0) ** n / math.factorial(2 * n + 1) for n in range(7)]
COS_TERMS = [(-1.0) ** n / math.factorial(2 * n) for n in range(8)]


def series(square, terms):
    value = jnp.full_like(square, terms[-1])
    for term in terms[-2::-1]:
        value = value * square + term
    return value


def basis_of(cycles):
    cycles = cycles - jnp.floor(cycles)
    turn = jnp.where(cycles >= 0.5, cycles - 1.0, cycles)
    angle = (2.0 * math.pi) * (jnp.abs(turn) - 0.25)
    square = angle * angle
    cosine = -angle * series(square, SIN_TERMS)
    size = series(square, COS_TERMS)
    sine = jnp.where(turn < 0.0, -size, size)
    return cosine, sine, 2.0 * cosine * cosine - 1.0, 2.0 * sine * cosine


def powers(by_cos, by_sin, cosine_two, sine_two, total, level):
    count = cosine_two.shape[0]
    cosine, sine = by_cos[:count], by_sin[:count]
    inverse = 1.0 / total
    mean_level = level * inverse
    ycos = by_cos[count:] - mean_level * cosine
    ysin = by_sin[count:] - mean_level * sine
    cc_term = 0.5 * (total + cosine_two) - cosine * cosine * inverse + RIDGE * total
    ss_term = 0.5 * (total - cosine_two) - sine * sine * inverse + RIDGE * total
    cs_term = 0.5 * sine_two - cosine * sine * inverse
    determinant = cc_term * ss_term - cs_term * cs_term
    return (
        ss_term * ycos * ycos + cc_term * ysin * ysin - 2.0 * cs_term * ycos * ysin
    ) / determinant


def per_device(light_curves, valid, pixel, inv_sigma, modes_init, epoch_jitter, freq_index):
    obj_n = lax.axis_size("obj")
    ep_n = lax.axis_size("ep")
    order = modes_init.shape[1]
    rows, cols = light_curves.shape
    share = rows // ep_n
    epochs = epoch_jitter.shape[0]
    pix_lanes = -(-4 * obj_n // LANES) * LANES
    near = [
        (do, de)
        for do in sorted({0, 1 % obj_n, (obj_n - 1) % obj_n}, reverse=True)
        for de in reversed(range(ep_n))
        if (do, de) != (0, 0)
    ]
    depth = sum(order - first_of(i) for i in range(order)) + order
    wide = -(-depth // LANES) * LANES
    phases = 2 * ITERS + 1
    vmem = pl.BlockSpec(memory_space=pltpu.VMEM)
    sem = pltpu.SemaphoreType.DMA
    count = freq_index.shape[0]
    parts = 4 * ITERS
    return pl.pallas_call(
        functools.partial(detrend_kernel, obj_n, ep_n, order, near),
        out_shape=(
            jax.ShapeDtypeStruct((rows, cols), F32),
            jax.ShapeDtypeStruct((share, count), F32),
        ),
        in_specs=[vmem] * 7,
        out_specs=(vmem,) * 2,
        scratch_shapes=[
            pltpu.VMEM((parts, 4, epochs, count // parts), jnp.bfloat16),
            pltpu.VMEM((epochs, LANES), F32),
            pltpu.VMEM((order, rows), F32),
            pltpu.VMEM((order, cols), F32),
            pltpu.VMEM((phases, SUB, pix_lanes), F32),
            pltpu.VMEM((phases, len(near), SUB, pix_lanes), F32),
            pltpu.VMEM((ITERS, depth, rows), F32),
            pltpu.VMEM((ITERS, max(ep_n - 1, 1), depth, rows), F32),
            pltpu.VMEM((ITERS, cols // SUB, SUB, wide), F32),
            pltpu.VMEM((ITERS, max(obj_n - 1, 1), SUB, wide), F32),
            pltpu.VMEM((ITERS, SUB, LANES), F32),
            pltpu.VMEM((ITERS, max(obj_n, cols // SUB), SUB, LANES), F32),
            pltpu.VMEM((2, rows, cols), jnp.bfloat16),
            pltpu.VMEM((ep_n, 2, share, cols), jnp.bfloat16),
            sem((2, phases, len(near))),
            sem((2, ITERS, max(ep_n - 1, 1))),
            sem((2, ITERS, max(obj_n - 1, 1))),
            sem((2, ITERS, max(obj_n - 1, 1))),
            sem((2, max(ep_n - 1, 1))),
        ],
        compiler_params=pltpu.CompilerParams(collective_id=0, has_side_effects=True),
    )(
        light_curves, valid, pixel[None], inv_sigma[None], modes_init.T,
        epoch_jitter[None], freq_index[None],
    )


def solution(mesh):
    in_specs = (P("obj", "ep"), P("obj", "ep"), P("obj"), P("obj"), P("ep", None), P(), P())
    out_specs = (P("obj", "ep"), P(("obj", "ep"), None))
    return jax.shard_map(
        per_device, mesh=mesh, in_specs=in_specs, out_specs=out_specs, check_vma=False
    )
```

profile of v0, /device:TPU:0, one launch (start us, length us, event | category | flops | bytes accessed | tf_op | source)
XLA Modules:
  0.0 66.1 jit_solution(1653840756131972785)
XLA Ops:
  0.6 62.1 %shard_map.86 = (f32[128,128]{1,0:T(8,128)}, f32[64,2048]{1,0:T(8,128)}) custom-call(f32[128,128]{1,0:T(8,128)} %lc_ref.1, s32[128,128]{1,0:T(8,128)} %valid_ref.1, s32[1,128]{1,0:T(1,128)} %bitcast.8, f32[1,128]{1,0:T(1,128)} %bitcast.9, f32[16,128]{1,0:T(8,128)} %bitcast.5, f32[1,256]{1,0:T(1,128)} %bitcast.7, s32[1,2048]{1,0:T(1,128)} %bitcast.6), custom_call_target="tpu_custom_call" | custom-call | tf_op jit(solution)/shard_map/pallas_call | solution.py:353
  62.8 1.5 %copy.11 = f32[128,128]{1,0:T(8,128)} copy(f32[128,128]{1,0:T(8,128)} %get-tuple-element.4) | data formatting | bytes 131072
  64.3 1.9 %copy.12 = f32[64,2048]{1,0:T(8,128)} copy(f32[64,2048]{1,0:T(8,128)} %get-tuple-element.5) | data formatting | bytes 1048576
where the time goes:
time: 66.4 us; the launch traced here: 66.1 us
  Pallas kernels  62.1 us (94%)
  local copies, waits for them, and re-layouts  3.34 us (5%)
    pallas_call x1, Pallas kernels, per_device(): pl.pallas_call(functools.partial(detrend_kernel, obj_n, ep_n, order, near...  62.1 us
    unnamed x2, local copies, waits for them, and re-layouts  3.34 us

commit v1 on v0

v1 whole, which is shorter than its diff:
```python
import functools
import math

import jax
import jax.numpy as jnp
from jax import lax
from jax.experimental import pallas as pl
from jax.experimental.pallas import tpu as pltpu
from jax.sharding import PartitionSpec as P

ITERS = 2


HUBER = 1.345
DAMP = 2.0
RIDGE = 0.05
HIGHEST = lax.Precision.HIGHEST
LANES = 128
SUB = 8
GROUP = 4
ABSENT = 1e30
F32 = jnp.float32
BF16 = jnp.bfloat16
STRIP = 32
MESH = pl.DeviceIdType.MESH


def halves(values):
    high = values.astype(BF16)
    return high, (values - high.astype(F32)).astype(BF16)


def cyclic_outer(vectors):
    order = vectors.shape[0]
    parts = [vectors * vectors]
    for shift in range(1, order // 2 + 1):
        turned = jnp.concatenate([vectors[shift:], vectors[:shift]], axis=0)
        part = vectors * turned
        parts.append(part if shift < order // 2 else part[: order // 2])
    return jnp.concatenate(parts, axis=0)


def cyclic_row(i, j, order):
    ahead = (j - i) % order
    if ahead == order // 2:
        return ahead * order + min(i, j)
    return ahead * order + i if ahead < order // 2 else (order - ahead) * order + j


def damped_solve(load, order):
    pairs = order * order // 2 + order // 2
    entry = {}
    for i in range(order):
        for j in range(i + 1):
            entry[i, j] = load(cyclic_row(i, j, order))
        entry[i, i] = entry[i, i] + DAMP
    remain = [load(pairs + i) for i in range(order)]
    inverse = []
    for k in range(order):
        inverse.append(1.0 / entry[k, k])
        for i in range(k + 1, order):
            scaled = entry[i, k] * inverse[k]
            for j in range(k + 1, i + 1):
                entry[i, j] = entry[i, j] - scaled * entry[j, k]
            remain[i] = remain[i] - scaled * remain[k]
    solved = [None] * order
    for k in reversed(range(order)):
        solved[k] = remain[k] * inverse[k]
        for j in range(k):
            remain[j] = remain[j] - entry[k, j] * solved[k]
    return solved


def as_column(row):
    return jnp.broadcast_to(row, (LANES, row.shape[1])).T


def detrend_kernel(
    obj_n, ep_n, order, lc_ref, valid_ref, pixel_ref, sigma_ref, modes_ref,
    jitter_ref, freq_ref, resid_ref, power_ref, basis_s, times_s,
    blk, halo_send, halo, first, lens, mens, sres, coef_s, modes_s, gram_s, tall_s,
    part_send, part_recv, solved_s, mode_send, mode_recv, final_s,
    near_sem, forward_sem, blk_sem, halo_out, halo_forward, halo_sem, first_sem,
    part_sem, mode_sem,
):
    me_o, me_e = lax.axis_index("obj"), lax.axis_index("ep")
    rows, cols = lc_ref.shape
    planes = obj_n // GROUP
    q, r = me_o // GROUP, lax.rem(me_o, GROUP)
    p, core = r // 2, lax.rem(r, 2)
    share = rows // ep_n
    epochs = cols * ep_n
    half = cols // 2
    tiles = GROUP + 1
    slab = cols // GROUP
    pairs = order * order // 2 + order // 2
    depth = pairs + order
    quarter = part_send.shape[1]
    pixels = 4 * obj_n

    def device(plane, chip, side, ep):
        return {"obj": plane * GROUP + chip * 2 + side, "ep": ep}

    def remote(src, dst, send, recv, where):
        return pltpu.make_async_remote_copy(
            src_ref=src, dst_ref=dst, send_sem=send, recv_sem=recv,
            device_id=where, device_id_type=MESH,
        )

    chips = [(dp, de) for dp in range(GROUP // 2) for de in range(ep_n)]
    inner = [(dr, de) for dr in range(GROUP) for de in range(ep_n) if (dr, de) != (0, 0)]

    def turned(dp, de):
        return lax.rem(p + dp, GROUP // 2), lax.rem(me_e + de, ep_n)

    has_prev, has_next = q > 0, q < planes - 1
    barrier = pltpu.get_barrier_semaphore()

    def greet(where):
        pl.semaphore_signal(barrier, inc=1, device_id=where, device_id_type=MESH)

    for dr, de in inner:
        greet({"obj": q * GROUP + lax.rem(r + dr, GROUP), "ep": lax.rem(me_e + de, ep_n)})
    for k in range(1, planes):
        greet({"obj": lax.rem(me_o + k * GROUP, obj_n), "ep": me_e})
    for there, exists in ((q - 1, has_prev), (q + 1, has_next)):
        @pl.when(exists)
        def _():
            for dp, de in chips:
                chip, ep = turned(dp, de)
                greet(device(there, chip, core, ep))

    width = basis_s.shape[3]
    times_s[...] = as_column(
        lax.broadcasted_iota(jnp.int32, (1, epochs), 1).astype(F32) + jitter_ref[...]
    )

    def fill_basis(block):
        begin = pl.multiple_of(block * width, width)
        freqs = (freq_ref[:, pl.ds(begin, width)] + 1).astype(F32) / (4.0 * epochs)

        def strip(step, carry):
            at = pl.ds(pl.multiple_of(step * STRIP, STRIP), STRIP)
            times = jnp.concatenate([times_s[at, :]] * (width // LANES), axis=1)
            for kind, values in enumerate(basis_of(times * freqs)):
                basis_s[block, kind, at, :] = values.astype(BF16)
            return carry

        lax.fori_loop(0, epochs // STRIP, strip, 0)

    blocks = basis_s.shape[0]
    lane = lax.broadcasted_iota(jnp.int32, (1, rows), 1)
    low_half = lane < rows // 2
    own = jnp.where(valid_ref[...] != 0, lc_ref[...], ABSENT).T
    marks = jnp.concatenate(
        [pixel_ref[...].astype(F32), sigma_ref[...], jnp.zeros((SUB - 2, rows), F32)], axis=0
    )
    mine = blk.at[me_e, r]
    blk[me_e, r, :cols] = own
    blk[me_e, r, cols:] = marks
    upper, lower = own[:half], own[half:]
    is_last = r == GROUP - 1
    turned_upper, turned_lower = pltpu.roll(upper, rows // 2, 1), pltpu.roll(lower, rows // 2, 1)
    halo_send[:half] = jnp.where(
        is_last,
        jnp.where(low_half, turned_upper, lower),
        jnp.where(low_half, upper, turned_lower),
    )
    halo_send[half:] = jnp.where(is_last, pltpu.roll(marks, rows // 2, 1), marks)
    first[me_e] = modes_ref[...]
    missing = jnp.concatenate(
        [jnp.full((half, rows), ABSENT, F32), jnp.full((1, rows), -1.0, F32),
         jnp.ones((SUB - 1, rows), F32)], axis=0,
    )
    for kind, exists in ((0, has_prev), (1, has_next)):
        @pl.when(jnp.logical_not(exists))
        def _():
            for ep in range(ep_n):
                halo[kind, ep] = missing

    def early(block, carry):
        fill_basis(block)
        return carry

    lax.fori_loop(0, blocks // 2, early, 0)
    pl.semaphore_wait(
        barrier,
        len(inner) + planes - 1 + len(chips) * (has_prev.astype(jnp.int32) + has_next.astype(jnp.int32)),
    )

    partner = device(q, p, 1 - core, me_e)
    near = []
    for n, (dp, de) in enumerate(chips):
        if (dp, de) != (0, 0):
            chip, ep = turned(dp, de)
            near.append(remote(mine, mine, near_sem.at[n], blk_sem.at[me_e, r], device(q, chip, core, ep)))
            near[-1].start()
    forwards = [remote(mine, mine, forward_sem.at[0], blk_sem.at[me_e, r], partner)]
    forwards[0].start()
    greetings = []
    for de in range(1, ep_n):
        greetings.append(remote(
            modes_ref, first.at[me_e], first_sem.at[0, de], first_sem.at[1, me_e],
            device(q, p, core, lax.rem(me_e + de, ep_n)),
        ))
        greetings[-1].start()

    halo_kinds = (
        (0, q + 1, jnp.logical_and(r == GROUP - 1, has_next), has_prev, core == 1),
        (1, q - 1, jnp.logical_and(r == 0, has_prev), has_next, core == 0),
    )

    def halo_copies(kind, there):
        made = []
        for n, (dp, de) in enumerate(chips):
            chip, ep = turned(dp, de)
            made.append(remote(
                halo_send, halo.at[kind, me_e], halo_out.at[n], halo_sem.at[kind, me_e],
                device(there, chip, core, ep),
            ))
        return made

    for kind, there, sends, _, _ in halo_kinds:
        @pl.when(sends)
        def _():
            for copy in halo_copies(kind, there):
                copy.start()

    def halo_step(kind, ep):
        slot = halo.at[kind, ep]
        return remote(slot, slot, halo_forward.at[ep], halo_sem.at[kind, ep], partner)

    for n, (dp, de) in enumerate(chips):
        if (dp, de) != (0, 0):
            chip, ep = turned(dp, de)
            slot = blk.at[ep, chip * 2 + core]
            forward = remote(slot, slot, forward_sem.at[n], blk_sem.at[ep, chip * 2 + core], partner)
            forward.wait_recv()
            forward.start()
            forwards.append(forward)
    for kind, _, _, arrives, passes in halo_kinds:
        @pl.when(jnp.logical_and(arrives, passes))
        def _():
            for ep in range(ep_n):
                step = halo_step(kind, ep)
                step.wait_recv()
                step.start()

    def late(block, carry):
        fill_basis(block)
        return carry

    lax.fori_loop(blocks // 2, blocks, late, 0)
    for dp, de in chips:
        chip, ep = turned(dp, de)
        slot = blk.at[ep, chip * 2 + 1 - core]
        remote(slot, slot, forward_sem.at[0], blk_sem.at[ep, chip * 2 + 1 - core], partner).wait_recv()
    for kind, _, _, arrives, passes in halo_kinds:
        @pl.when(jnp.logical_and(arrives, jnp.logical_not(passes)))
        def _():
            for ep in range(ep_n):
                halo_step(kind, ep).wait_recv()
    for de in range(1, ep_n):
        ep = lax.rem(me_e + de, ep_n)
        remote(modes_ref, first.at[ep], first_sem.at[0, de], first_sem.at[1, ep], partner).wait_recv()
    for copy in near + forwards + greetings:
        copy.wait_send()
    for kind, there, sends, _, _ in halo_kinds:
        @pl.when(sends)
        def _():
            for copy in halo_copies(kind, there):
                copy.wait_send()
    for kind, _, _, arrives, passes in halo_kinds:
        @pl.when(jnp.logical_and(arrives, passes))
        def _():
            for ep in range(ep_n):
                halo_step(kind, ep).wait_send()

    pixel_level = lax.broadcasted_iota(jnp.int32, (pixels, rows), 0).astype(F32)
    marked = [blk[0, t, cols:] for t in range(GROUP)]
    before, after = halo[0, 0, half:], pltpu.roll(halo[1, 0, half:], rows // 2, 1)
    marked.append(jnp.where(low_half, before, after))
    pixel_row = [m[0:1] for m in marked]
    sigma_row = [m[1:2] for m in marked]
    totals = []
    for t in range(tiles):
        total = jnp.zeros((1, rows), F32)
        for ep in range(ep_n):
            if t < GROUP:
                value = blk[ep, t, :cols]
            else:
                prev, follow = halo[0, ep, :half], halo[1, ep, :half]
                value = jnp.concatenate([
                    jnp.where(low_half, prev, pltpu.roll(follow, rows // 2, 1)),
                    jnp.where(low_half, pltpu.roll(prev, rows // 2, 1), follow),
                ], axis=0)
            seen = value < 0.5 * ABSENT
            scale = jnp.where(seen, sigma_row[t], 0.0)
            at = slice(ep * cols, (ep + 1) * cols)
            mens[t, at] = scale
            lens[t, at] = value * scale
            total = total + jnp.sum(seen.astype(F32), axis=0, keepdims=True)
        totals.append(total)

    def by_pixel(tile_rows, tile_pixels):
        gathered = jnp.zeros((pixels, rows), F32)
        for row, where in zip(tile_rows, tile_pixels):
            gathered = gathered + jnp.where(where == pixel_level, row, 0.0)
        return jnp.sum(gathered, axis=1, keepdims=True)

    inverse_count = 1.0 / jnp.maximum(by_pixel(totals, pixel_row), 1.0)

    def limits(squares, tile_pixels, wanted):
        sums = by_pixel(squares, tile_pixels)
        spread = HUBER * jnp.sqrt(sums * inverse_count + 1e-06)
        return [
            jnp.maximum(
                jnp.sum(jnp.where(where == pixel_level, spread, 0.0), axis=0, keepdims=True), 1e-3
            )
            for where in wanted
        ]

    def modes_factor():
        high, low = halves(modes_s[...])
        stacked = jnp.concatenate([high, high, low], axis=0).astype(F32)
        stacked = jnp.concatenate(
            [stacked, jnp.zeros((LANES - 3 * order, epochs), F32)], axis=0
        )
        tall_s[...] = stacked.T.astype(BF16)

    def fitted(coef):
        high, low = halves(coef)
        wide = jnp.concatenate(
            [high, low, high, jnp.zeros((LANES - 3 * order, coef.shape[1]), BF16)], axis=0
        )
        return jnp.dot(tall_s[...], wide, preferred_element_type=F32)

    def scaled_residuals():
        squares = []
        for t in range(tiles):
            left = lens[t] - mens[t] * fitted(coef_s[t * order : (t + 1) * order])
            sres[t] = left
            squares.append(jnp.sum(left * left, axis=0, keepdims=True))
        return squares

    def reach(left, limit, sigma):
        return (sigma * limit) / jnp.maximum(jnp.abs(left), limit)

    coef_s[...] = jnp.zeros_like(coef_s)
    for ep in range(ep_n):
        modes_s[:, ep * cols : (ep + 1) * cols] = first[ep]
    modes_factor()

    def iteration(it, carry):
        limit = limits(scaled_residuals(), pixel_row, pixel_row)
        modes = modes_s[...]
        outer_high, outer_low = halves(cyclic_outer(modes))
        modes_high, modes_low = halves(modes)
        for t in range(tiles):
            factor = reach(sres[t], limit[t], sigma_row[t])
            weight = (mens[t] * factor).astype(BF16)
            value_high, value_low = halves(lens[t] * factor)
            gram = jnp.dot(outer_high, weight, preferred_element_type=F32)
            gram = gram + jnp.dot(outer_low, weight, preferred_element_type=F32)
            target = jnp.dot(modes_high, value_high, preferred_element_type=F32)
            target = target + jnp.dot(modes_low, value_high, preferred_element_type=F32)
            target = target + jnp.dot(modes_high, value_low, preferred_element_type=F32)
            gram_s[t * depth : t * depth + pairs] = gram
            gram_s[t * depth + pairs : (t + 1) * depth] = target
        solved = damped_solve(lambda row: gram_s[pl.ds(row, tiles, stride=depth), :], order)
        for k in range(order):
            coef_s[pl.ds(k, tiles, stride=order), :] = solved[k]

        limit = limits(scaled_residuals(), pixel_row, pixel_row[:GROUP])
        at = pl.ds(pl.multiple_of(me_e * cols + r * slab, slab), slab)
        weights, value_highs, value_lows, outers, coefs = [], [], [], [], []
        for t in range(GROUP):
            factor = reach(sres[t, at], limit[t], sigma_row[t])
            weights.append((mens[t, at] * factor).astype(BF16))
            value_high, value_low = halves(lens[t, at] * factor)
            value_highs.append(value_high)
            value_lows.append(value_low)
            coef = coef_s[t * order : (t + 1) * order]
            outers.append(halves(cyclic_outer(coef)))
            coefs.append(halves(coef))

        def copied(parts):
            return jnp.concatenate([jnp.concatenate(parts, axis=1)] * GROUP, axis=0)

        def across(left, right):
            return lax.dot_general(
                left, right, (((1,), (1,)), ((), ())), preferred_element_type=F32
            )

        weight, value_high, value_low = copied(weights), copied(value_highs), copied(value_lows)
        outer_high = jnp.concatenate([pair[0] for pair in outers], axis=1)
        outer_low = jnp.concatenate([pair[1] for pair in outers], axis=1)
        coef_high = jnp.concatenate([pair[0] for pair in coefs], axis=1)
        coef_low = jnp.concatenate([pair[1] for pair in coefs], axis=1)
        gram = across(outer_high, weight) + across(outer_low, weight)
        target = across(coef_high, value_high) + across(coef_low, value_high)
        target = target + across(coef_high, value_low)
        whole = jnp.concatenate(
            [gram, target, jnp.zeros((GROUP * quarter - depth, rows), F32)], axis=0
        )
        packed = whole[:quarter]
        for k in range(1, GROUP):
            packed = jnp.where(lane >= k * slab, whole[k * quarter : (k + 1) * quarter], packed)
        part_send[it] = packed
        copies = []
        for k in range(1, planes):
            copies.append(remote(
                part_send.at[it], part_recv.at[it, k - 1],
                part_sem.at[0, it, k - 1], part_sem.at[1, it, k - 1],
                {"obj": lax.rem(me_o + k * GROUP, obj_n), "ep": me_e},
            ))
            copies[-1].start()
        for k in range(1, planes):
            copies[k - 1].wait()
            packed = packed + part_recv[it, k - 1]
        gram_s[:quarter] = packed
        for k in range(1, GROUP):
            gram_s[k * quarter : (k + 1) * quarter] = pltpu.roll(packed, rows - k * slab, 1)
        solved = damped_solve(lambda row: gram_s[row : row + 1, :], order)
        for k in range(order):
            solved_s[k : k + 1] = solved[k]
        fresh = pltpu.roll(solved_s[...], r * slab, 1)
        mode_send[it] = fresh
        mode_recv[it, me_e, r] = fresh
        copies = []
        for n, (dr, de) in enumerate(inner):
            copies.append(remote(
                mode_send.at[it], mode_recv.at[it, me_e, r],
                mode_sem.at[0, it, n], mode_sem.at[1, it, n],
                {"obj": q * GROUP + lax.rem(r + dr, GROUP), "ep": lax.rem(me_e + de, ep_n)},
            ))
            copies[-1].start()
        for copy in copies:
            copy.wait()
        for ep in range(ep_n):
            joined = mode_recv[it, ep, 0]
            for k in range(1, GROUP):
                joined = jnp.where(lane >= k * slab, mode_recv[it, ep, k], joined)
            modes_s[:, ep * cols : (ep + 1) * cols] = joined
        modes_factor()
        return carry

    lax.fori_loop(0, ITERS, iteration, 0)
    own_coef = coef_s[pl.ds(pl.multiple_of(r * order, order), order), :]
    beside = jnp.where(
        me_e < ep_n // 2, jnp.where(r == 0, GROUP, r - 1), r + 1
    )
    side_coef = coef_s[pl.ds(pl.multiple_of(beside * order, order), order), :]
    both_pixels, squares = [], []
    lefts = []
    for t, coef in ((r, own_coef), (beside, side_coef)):
        left = lens[t] - mens[t] * fitted(coef)
        lefts.append(left)
        squares.append(jnp.sum(left * left, axis=0, keepdims=True))
    for t, name in ((r, 0), (beside, 1)):
        chosen = pixel_row[0]
        for k in range(1, tiles):
            chosen = jnp.where(t == k, pixel_row[k], chosen)
        both_pixels.append(chosen)
    own_sigma = sigma_ref[...]
    (limit,) = limits(squares, both_pixels, both_pixels[:1])
    factor = reach(lefts[0], limit, own_sigma)
    final_s[0] = (mens[r] * factor).T.astype(BF16)
    final_s[1] = (lefts[0] * factor).T.astype(BF16)
    own_modes = modes_s[:, pl.ds(pl.multiple_of(me_e * cols, cols), cols)]
    resid_ref[...] = lc_ref[...] - lax.dot_general(
        own_coef, own_modes, (((0,), (0,)), ((), ())),
        precision=HIGHEST, preferred_element_type=F32,
    )
    mine_at = pl.ds(pl.multiple_of(me_e * share, share), share)
    weights, values = final_s[0, mine_at, :], final_s[1, mine_at, :]
    both = jnp.concatenate([weights, values], axis=0)
    total = jnp.sum(weights.astype(F32), axis=1, keepdims=True)
    level = jnp.sum(values.astype(F32), axis=1, keepdims=True)

    def spectrum(block, carry):
        at = pl.ds(pl.multiple_of(block * width, width), width)
        power_ref[:, at] = powers(
            jnp.dot(both, basis_s[block, 0], preferred_element_type=F32),
            jnp.dot(both, basis_s[block, 1], preferred_element_type=F32),
            jnp.dot(weights, basis_s[block, 2], preferred_element_type=F32),
            jnp.dot(weights, basis_s[block, 3], preferred_element_type=F32),
            total,
            level,
        )
        return carry

    lax.fori_loop(0, blocks, spectrum, 0)


SIN_TERMS = [(-1.0) ** n / math.factorial(2 * n + 1) for n in range(7)]
COS_TERMS = [(-1.0) ** n / math.factorial(2 * n) for n in range(8)]


def series(square, terms):
    value = jnp.full_like(square, terms[-1])
    for term in terms[-2::-1]:
        value = value * square + term
    return value


def basis_of(cycles):
    cycles = cycles - jnp.floor(cycles)
    turn = jnp.where(cycles >= 0.5, cycles - 1.0, cycles)
    angle = (2.0 * math.pi) * (jnp.abs(turn) - 0.25)
    square = angle * angle
    cosine = -angle * series(square, SIN_TERMS)
    size = series(square, COS_TERMS)
    sine = jnp.where(turn < 0.0, -size, size)
    return cosine, sine, 2.0 * cosine * cosine - 1.0, 2.0 * sine * cosine


def powers(by_cos, by_sin, cosine_two, sine_two, total, level):
    count = cosine_two.shape[0]
    cosine, sine = by_cos[:count], by_sin[:count]
    inverse = 1.0 / total
    mean_level = level * inverse
    ycos = by_cos[count:] - mean_level * cosine
    ysin = by_sin[count:] - mean_level * sine
    cc_term = 0.5 * (total + cosine_two) - cosine * cosine * inverse + RIDGE * total
    ss_term = 0.5 * (total - cosine_two) - sine * sine * inverse + RIDGE * total
    cs_term = 0.5 * sine_two - cosine * sine * inverse
    determinant = cc_term * ss_term - cs_term * cs_term
    return (
        ss_term * ycos * ycos + cc_term * ysin * ysin - 2.0 * cs_term * ycos * ysin
    ) / determinant


def per_device(light_curves, valid, pixel, inv_sigma, modes_init, epoch_jitter, freq_index):
    obj_n = lax.axis_size("obj")
    ep_n = lax.axis_size("ep")
    order = modes_init.shape[1]
    rows, cols = light_curves.shape
    share = rows // ep_n
    epochs = epoch_jitter.shape[0]
    planes = obj_n // GROUP
    tiles = GROUP + 1
    half = cols // 2
    depth = order * order // 2 + order // 2 + order
    quarter = -(-depth // (GROUP * SUB)) * SUB
    chips = GROUP // 2 * ep_n
    inner = GROUP * ep_n - 1
    vmem = pl.BlockSpec(memory_space=pltpu.VMEM)
    sem = pltpu.SemaphoreType.DMA
    count = freq_index.shape[0]
    parts = 4 * ITERS
    return pl.pallas_call(
        functools.partial(detrend_kernel, obj_n, ep_n, order),
        out_shape=(
            jax.ShapeDtypeStruct((rows, cols), F32),
            jax.ShapeDtypeStruct((share, count), F32),
        ),
        in_specs=[vmem] * 7,
        out_specs=(vmem,) * 2,
        scratch_shapes=[
            pltpu.VMEM((parts, 4, epochs, count // parts), BF16),
            pltpu.VMEM((epochs, LANES), F32),
            pltpu.VMEM((ep_n, GROUP, cols + SUB, rows), F32),
            pltpu.VMEM((half + SUB, rows), F32),
            pltpu.VMEM((2, ep_n, half + SUB, rows), F32),
            pltpu.VMEM((ep_n, order, cols), F32),
            pltpu.VMEM((tiles, epochs, rows), F32),
            pltpu.VMEM((tiles, epochs, rows), F32),
            pltpu.VMEM((tiles, epochs, rows), F32),
            pltpu.VMEM((tiles * order, rows), F32),
            pltpu.VMEM((order, epochs), F32),
            pltpu.VMEM((tiles * depth, rows), F32),
            pltpu.VMEM((epochs, LANES), BF16),
            pltpu.VMEM((ITERS, quarter, rows), F32),
            pltpu.VMEM((ITERS, planes - 1, quarter, rows), F32),
            pltpu.VMEM((order, rows), F32),
            pltpu.VMEM((ITERS, order, rows), F32),
            pltpu.VMEM((ITERS, ep_n, GROUP, order, rows), F32),
            pltpu.VMEM((2, rows, epochs), BF16),
            sem((chips,)),
            sem((chips,)),
            sem((ep_n, GROUP)),
            sem((chips,)),
            sem((ep_n,)),
            sem((2, ep_n)),
            sem((2, ep_n)),
            sem((2, ITERS, planes - 1)),
            sem((2, ITERS, inner)),
        ],
        compiler_params=pltpu.CompilerParams(collective_id=0, has_side_effects=True),
    )(
        light_curves, valid, pixel[None], inv_sigma[None], modes_init.T,
        epoch_jitter[None], freq_index[None],
    )


def solution(mesh):
    in_specs = (P("obj", "ep"), P("obj", "ep"), P("obj"), P("obj"), P("ep", None), P(), P())
    out_specs = (P("obj", "ep"), P(("obj", "ep"), None))
    return jax.shard_map(
        per_device, mesh=mesh, in_specs=in_specs, out_specs=out_specs, check_vma=False
    )
```

time: 66.4 us -> 42.2 us (0.64)
  Pallas kernels: 62.1 us -> 37.9 us
    pallas_call x1, Pallas kernels: 62.1 us -> 37.9 us  [per_device(): pl.pallas_call(functools.partial(detrend_kernel, obj_n, ep_n, order), out...]
where the time goes in v1:
time: 42.2 us; the launch traced here: 41.9 us
  Pallas kernels  37.9 us (90%)
  local copies, waits for them, and re-layouts  3.34 us (8%)
  between operations  0.64 us (2%)
    pallas_call x1, Pallas kernels, per_device(): pl.pallas_call(functools.partial(detrend_kernel, obj_n, ep_n, order), out...  37.9 us
    unnamed x2, local copies, waits for them, and re-layouts  3.34 us

profile of v1, /device:TPU:0, one launch (start us, length us, event | category | flops | bytes accessed | tf_op | source)
XLA Modules:
  0.0 41.9 jit_solution(5330947891982458572)
XLA Ops:
  0.6 37.9 %shard_map.86 = (f32[128,128]{1,0:T(8,128)}, f32[64,2048]{1,0:T(8,128)}) custom-call(f32[128,128]{1,0:T(8,128)} %lc_ref.1, s32[128,128]{1,0:T(8,128)} %valid_ref.1, s32[1,128]{1,0:T(1,128)} %bitcast.8, f32[1,128]{1,0:T(1,128)} %bitcast.9, f32[16,128]{1,0:T(8,128)} %bitcast.5, f32[1,256]{1,0:T(1,128)} %bitcast.7, s32[1,2048]{1,0:T(1,128)} %bitcast.6), custom_call_target="tpu_custom_call" | custom-call | tf_op jit(solution)/shard_map/pallas_call | solution.py:552
  38.6 1.5 %copy.11 = f32[128,128]{1,0:T(8,128)} copy(f32[128,128]{1,0:T(8,128)} %get-tuple-element.4) | data formatting | bytes 131072
  40.0 1.9 %copy.12 = f32[64,2048]{1,0:T(8,128)} copy(f32[64,2048]{1,0:T(8,128)} %get-tuple-element.5) | data formatting | bytes 1048576

commit v2 on v1

--- a/solution.py
+++ b/solution.py
@@ -17,6 +17,8 @@
 HIGHEST = lax.Precision.HIGHEST
 LANES = 128
 SUB = 8
+UNROLL = 2
+ROOM = 24 << 20
 GROUP = 4
 ABSENT = 1e30
 F32 = jnp.float32
@@ -76,11 +78,12 @@
 
 
 def detrend_kernel(
-    obj_n, ep_n, order, lc_ref, valid_ref, pixel_ref, sigma_ref, modes_ref,
-    jitter_ref, freq_ref, resid_ref, power_ref, basis_s, times_s,
+    obj_n, ep_n, order, lc_hbm, valid_hbm, pixel_hbm, sigma_hbm, modes_hbm,
+    jitter_hbm, freq_hbm, resid_ref, ready_ref, basis_s,
+    lc_ref, valid_ref, pixel_ref, sigma_ref, jitter_ref, freq_ref, times_s,
     blk, halo_send, halo, first, lens, mens, sres, coef_s, modes_s, gram_s, tall_s,
     part_send, part_recv, solved_s, mode_send, mode_recv, final_s,
-    near_sem, forward_sem, blk_sem, halo_out, halo_forward, halo_sem, first_sem,
+    load_sem, near_sem, forward_sem, blk_sem, halo_out, halo_forward, halo_sem, first_sem,
     part_sem, mode_sem,
 ):
     me_o, me_e = lax.axis_index("obj"), lax.axis_index("ep")
@@ -107,7 +110,10 @@
             device_id=where, device_id_type=MESH,
         )
 
-    chips = [(dp, de) for dp in range(GROUP // 2) for de in range(ep_n)]
+    chips = sorted(
+        ((dp, de) for dp in range(GROUP // 2) for de in range(ep_n)),
+        key=lambda step: (min(step[0], 1) + min(step[1], 1)) % 3 * -1,
+    )
     inner = [(dr, de) for dr in range(GROUP) for de in range(ep_n) if (dr, de) != (0, 0)]
 
     def turned(dp, de):
@@ -130,6 +136,19 @@
                 chip, ep = turned(dp, de)
                 greet(device(there, chip, core, ep))
 
+    loads = [
+        pltpu.make_async_copy(source, target, load_sem.at[n])
+        for n, (source, target) in enumerate((
+            (lc_hbm, lc_ref), (valid_hbm, valid_ref), (pixel_hbm, pixel_ref),
+            (sigma_hbm, sigma_ref), (modes_hbm, first.at[me_e]), (jitter_hbm, jitter_ref),
+            (freq_hbm, freq_ref),
+        ))
+    ]
+    for load in loads:
+        load.start()
+    for load in loads:
+        load.wait()
+
     width = basis_s.shape[3]
     times_s[...] = as_column(
         lax.broadcasted_iota(jnp.int32, (1, epochs), 1).astype(F32) + jitter_ref[...]
@@ -167,7 +186,6 @@
         jnp.where(low_half, upper, turned_lower),
     )
     halo_send[half:] = jnp.where(is_last, pltpu.roll(marks, rows // 2, 1), marks)
-    first[me_e] = modes_ref[...]
     missing = jnp.concatenate(
         [jnp.full((half, rows), ABSENT, F32), jnp.full((1, rows), -1.0, F32),
          jnp.ones((SUB - 1, rows), F32)], axis=0,
@@ -200,7 +218,7 @@
     greetings = []
     for de in range(1, ep_n):
         greetings.append(remote(
-            modes_ref, first.at[me_e], first_sem.at[0, de], first_sem.at[1, me_e],
+            first.at[me_e], first.at[me_e], first_sem.at[0, de], first_sem.at[1, me_e],
             device(q, p, core, lax.rem(me_e + de, ep_n)),
         ))
         greetings[-1].start()
@@ -262,7 +280,7 @@
                 halo_step(kind, ep).wait_recv()
     for de in range(1, ep_n):
         ep = lax.rem(me_e + de, ep_n)
-        remote(modes_ref, first.at[ep], first_sem.at[0, de], first_sem.at[1, ep], partner).wait_recv()
+        remote(first.at[ep], first.at[ep], first_sem.at[0, de], first_sem.at[1, ep], partner).wait_recv()
     for copy in near + forwards + greetings:
         copy.wait_send()
     for kind, there, sends, _, _ in halo_kinds:
@@ -358,10 +376,11 @@
         modes_high, modes_low = halves(modes)
         for t in range(tiles):
             factor = reach(sres[t], limit[t], sigma_row[t])
-            weight = (mens[t] * factor).astype(BF16)
+            weight, weight_low = halves(mens[t] * factor)
             value_high, value_low = halves(lens[t] * factor)
             gram = jnp.dot(outer_high, weight, preferred_element_type=F32)
             gram = gram + jnp.dot(outer_low, weight, preferred_element_type=F32)
+            gram = gram + jnp.dot(outer_high, weight_low, preferred_element_type=F32)
             target = jnp.dot(modes_high, value_high, preferred_element_type=F32)
             target = target + jnp.dot(modes_low, value_high, preferred_element_type=F32)
             target = target + jnp.dot(modes_high, value_low, preferred_element_type=F32)
@@ -373,10 +392,12 @@
 
         limit = limits(scaled_residuals(), pixel_row, pixel_row[:GROUP])
         at = pl.ds(pl.multiple_of(me_e * cols + r * slab, slab), slab)
-        weights, value_highs, value_lows, outers, coefs = [], [], [], [], []
+        weights, weight_lows, value_highs, value_lows, outers, coefs = [], [], [], [], [], []
         for t in range(GROUP):
             factor = reach(sres[t, at], limit[t], sigma_row[t])
-            weights.append((mens[t, at] * factor).astype(BF16))
+            weight, weight_low = halves(mens[t, at] * factor)
+            weights.append(weight)
+            weight_lows.append(weight_low)
             value_high, value_low = halves(lens[t, at] * factor)
             value_highs.append(value_high)
             value_lows.append(value_low)
@@ -392,12 +413,14 @@
                 left, right, (((1,), (1,)), ((), ())), preferred_element_type=F32
             )
 
-        weight, value_high, value_low = copied(weights), copied(value_highs), copied(value_lows)
+        weight, weight_low = copied(weights), copied(weight_lows)
+        value_high, value_low = copied(value_highs), copied(value_lows)
         outer_high = jnp.concatenate([pair[0] for pair in outers], axis=1)
         outer_low = jnp.concatenate([pair[1] for pair in outers], axis=1)
         coef_high = jnp.concatenate([pair[0] for pair in coefs], axis=1)
         coef_low = jnp.concatenate([pair[1] for pair in coefs], axis=1)
         gram = across(outer_high, weight) + across(outer_low, weight)
+        gram = gram + across(outer_high, weight_low)
         target = across(coef_high, value_high) + across(coef_low, value_high)
         target = target + across(coef_high, value_low)
         whole = jnp.concatenate(
@@ -473,24 +496,38 @@
         precision=HIGHEST, preferred_element_type=F32,
     )
     mine_at = pl.ds(pl.multiple_of(me_e * share, share), share)
-    weights, values = final_s[0, mine_at, :], final_s[1, mine_at, :]
+    ready_ref[...] = final_s[:, mine_at, :]
+
+
+def spectrum_kernel(left_ref, ready_ref, basis_ref, resid_hbm, power_hbm, power_s, sems):
+    weights, values = ready_ref[0], ready_ref[1]
+    blocks, width = power_s.shape[0], power_s.shape[2]
+    kept = pltpu.make_async_copy(left_ref, resid_hbm, sems.at[blocks])
+    kept.start()
     both = jnp.concatenate([weights, values], axis=0)
     total = jnp.sum(weights.astype(F32), axis=1, keepdims=True)
     level = jnp.sum(values.astype(F32), axis=1, keepdims=True)
 
+    def out(block):
+        at = pl.ds(pl.multiple_of(block * width, width), width)
+        return pltpu.make_async_copy(power_s.at[block], power_hbm.at[:, at], sems.at[block])
+
     def spectrum(block, carry):
-        at = pl.ds(pl.multiple_of(block * width, width), width)
-        power_ref[:, at] = powers(
-            jnp.dot(both, basis_s[block, 0], preferred_element_type=F32),
-            jnp.dot(both, basis_s[block, 1], preferred_element_type=F32),
-            jnp.dot(weights, basis_s[block, 2], preferred_element_type=F32),
-            jnp.dot(weights, basis_s[block, 3], preferred_element_type=F32),
+        power_s[block] = powers(
+            jnp.dot(both, basis_ref[block, 0], preferred_element_type=F32),
+            jnp.dot(both, basis_ref[block, 1], preferred_element_type=F32),
+            jnp.dot(weights, basis_ref[block, 2], preferred_element_type=F32),
+            jnp.dot(weights, basis_ref[block, 3], preferred_element_type=F32),
             total,
             level,
         )
+        out(block).start()
         return carry
 
-    lax.fori_loop(0, blocks, spectrum, 0)
+    lax.fori_loop(0, blocks, spectrum, 0, unroll=UNROLL)
+    kept.wait()
+    for block in range(blocks):
+        out(block).wait()
 
 
 SIN_TERMS = [(-1.0) ** n / math.factorial(2 * n + 1) for n in range(7)]
@@ -546,19 +583,26 @@
     chips = GROUP // 2 * ep_n
     inner = GROUP * ep_n - 1
     vmem = pl.BlockSpec(memory_space=pltpu.VMEM)
+    hbm = pl.BlockSpec(memory_space=pltpu.HBM)
     sem = pltpu.SemaphoreType.DMA
     count = freq_index.shape[0]
     parts = 4 * ITERS
-    return pl.pallas_call(
+    left, ready, basis = pl.pallas_call(
         functools.partial(detrend_kernel, obj_n, ep_n, order),
         out_shape=(
             jax.ShapeDtypeStruct((rows, cols), F32),
-            jax.ShapeDtypeStruct((share, count), F32),
+            jax.ShapeDtypeStruct((2, share, epochs), BF16),
+            jax.ShapeDtypeStruct((parts, 4, epochs, count // parts), BF16),
         ),
-        in_specs=[vmem] * 7,
-        out_specs=(vmem,) * 2,
+        in_specs=[hbm] * 7,
+        out_specs=(vmem,) * 3,
         scratch_shapes=[
-            pltpu.VMEM((parts, 4, epochs, count // parts), BF16),
+            pltpu.VMEM((rows, cols), F32),
+            pltpu.VMEM((rows, cols), jnp.int32),
+            pltpu.VMEM((1, rows), jnp.int32),
+            pltpu.VMEM((1, rows), F32),
+            pltpu.VMEM((1, epochs), F32),
+            pltpu.VMEM((1, count), jnp.int32),
             pltpu.VMEM((epochs, LANES), F32),
             pltpu.VMEM((ep_n, GROUP, cols + SUB, rows), F32),
             pltpu.VMEM((half + SUB, rows), F32),
@@ -577,6 +621,7 @@
             pltpu.VMEM((ITERS, order, rows), F32),
             pltpu.VMEM((ITERS, ep_n, GROUP, order, rows), F32),
             pltpu.VMEM((2, rows, epochs), BF16),
+            sem((7,)),
             sem((chips,)),
             sem((chips,)),
             sem((ep_n, GROUP)),
@@ -587,11 +632,29 @@
             sem((2, ITERS, planes - 1)),
             sem((2, ITERS, inner)),
         ],
-        compiler_params=pltpu.CompilerParams(collective_id=0, has_side_effects=True),
+        compiler_params=pltpu.CompilerParams(
+            collective_id=0, has_side_effects=True, vmem_limit_bytes=ROOM
+        ),
     )(
-        light_curves, valid, pixel[None], inv_sigma[None], modes_init.T,
-        epoch_jitter[None], freq_index[None],
-    )
+        *(pltpu.with_memory_space_constraint(given, pltpu.HBM) for given in (
+            light_curves, valid, pixel[None], inv_sigma[None], modes_init.T,
+            epoch_jitter[None], freq_index[None],
+        ))
+    )
+    return pl.pallas_call(
+        spectrum_kernel,
+        out_shape=(
+            jax.ShapeDtypeStruct((rows, cols), F32),
+            jax.ShapeDtypeStruct((share, count), F32),
+        ),
+        in_specs=[vmem] * 3,
+        out_specs=(hbm,) * 2,
+        scratch_shapes=[
+            pltpu.VMEM((parts, share, count // parts), F32),
+            sem((parts + 1,)),
+        ],
+        compiler_params=pltpu.CompilerParams(vmem_limit_bytes=ROOM // 2),
+    )(left, ready, basis)
 
 
 def solution(mesh):

time: 42.2 us -> 37.4 us (0.89)
  local copies, waits for them, and re-layouts: 3.34 us -> 0 us
  Pallas kernels: 37.9 us -> 36.6 us
    pallas_call x1, Pallas kernels: 37.9 us -> 34.3 us  [per_device(): pl.pallas_call(functools.partial(detrend_kernel, obj_n, ep_n, order), out...]
    unnamed x2 -> x0, local copies, waits for them, and re-layouts: 3.34 us -> none
    pallas_call x0 -> x1, Pallas kernels: none -> 2.28 us  [per_device(): pl.pallas_call(spectrum_kernel, out_shape=(jax.ShapeDtypeStruct((rows, co...]
where the time goes in v2:
time: 37.4 us; the launch traced here: 37.2 us
  Pallas kernels  36.6 us (98%)
  between operations  0.64 us (2%)
    pallas_call x1, Pallas kernels, per_device(): pl.pallas_call(functools.partial(detrend_kernel, obj_n, ep_n, order), out...  34.3 us
    pallas_call x1, Pallas kernels, per_device(): pl.pallas_call(spectrum_kernel, out_shape=(jax.ShapeDtypeStruct((rows, co...  2.28 us

profile of v2, /device:TPU:0, one launch (start us, length us, event | category | flops | bytes accessed | tf_op | source)
XLA Modules:
  0.0 37.2 jit_solution(2378564556062924677)
XLA Ops:
  0.6 34.3 %shard_map.86 = (f32[128,128]{1,0:T(8,128)S(1)}, bf16[2,64,256]{2,1,0:T(8,128)(2,1)S(1)}, bf16[8,4,256,256]{3,2,1,0:T(8,128)(2,1)S(1)}) custom-call(f32[128,128]{1,0:T(8,128)} %lc_hbm.1, s32[128,128]{1,0:T(8,128)} %valid_hbm.1, s32[1,128]{1,0:T(1,128)} %bitcast.8, f32[1,128]{1,0:T(1,128)} %bitcast.9, f32[16,128]{1,0:T(8,128)} %bitcast.5, f32[1,256]{1,0:T(1,128)} %bitcast.7, ...), custom_call_target="tpu_custom_call" | custom-call | tf_op jit(solution)/shard_map/pallas_call | solution.py:590
  34.9 2.3 %shard_map.87 = (f32[128,128]{1,0:T(8,128)}, f32[64,2048]{1,0:T(8,128)}) custom-call(f32[128,128]{1,0:T(8,128)S(1)} %get-tuple-element.5.left_ref, bf16[2,64,256]{2,1,0:T(8,128)(2,1)S(1)} %get-tuple-element.6.ready_ref, bf16[8,4,256,256]{3,2,1,0:T(8,128)(2,1)S(1)} %get-tuple-element.7.basis_ref), custom_call_target="tpu_custom_call" | custom-call | tf_op jit(solution)/shard_map/pallas_call | solution.py:644

commit v3 on v2

--- a/solution.py
+++ b/solution.py
@@ -17,7 +17,7 @@
 HIGHEST = lax.Precision.HIGHEST
 LANES = 128
 SUB = 8
-UNROLL = 2
+UNROLL = 4
 ROOM = 24 << 20
 GROUP = 4
 ABSENT = 1e30
@@ -57,20 +57,19 @@
             entry[i, j] = load(cyclic_row(i, j, order))
         entry[i, i] = entry[i, i] + DAMP
     remain = [load(pairs + i) for i in range(order)]
-    inverse = []
+    factor = {}
     for k in range(order):
-        inverse.append(1.0 / entry[k, k])
+        inverse = 1.0 / entry[k, k]
         for i in range(k + 1, order):
-            scaled = entry[i, k] * inverse[k]
+            factor[i, k] = entry[i, k] * inverse
             for j in range(k + 1, i + 1):
-                entry[i, j] = entry[i, j] - scaled * entry[j, k]
-            remain[i] = remain[i] - scaled * remain[k]
-    solved = [None] * order
+                entry[i, j] = entry[i, j] - factor[i, k] * entry[j, k]
+            remain[i] = remain[i] - factor[i, k] * remain[k]
+        remain[k] = remain[k] * inverse
     for k in reversed(range(order)):
-        solved[k] = remain[k] * inverse[k]
         for j in range(k):
-            remain[j] = remain[j] - entry[k, j] * solved[k]
-    return solved
+            remain[j] = remain[j] - factor[k, j] * remain[k]
+    return remain
 
 
 def as_column(row):
@@ -200,7 +199,7 @@
         fill_basis(block)
         return carry
 
-    lax.fori_loop(0, blocks // 2, early, 0)
+    lax.fori_loop(0, blocks // 4, early, 0)
     pl.semaphore_wait(
         barrier,
         len(inner) + planes - 1 + len(chips) * (has_prev.astype(jnp.int32) + has_next.astype(jnp.int32)),
@@ -244,6 +243,12 @@
             for copy in halo_copies(kind, there):
                 copy.start()
 
+    def late(block, carry):
+        fill_basis(block)
+        return carry
+
+    lax.fori_loop(blocks // 4, blocks // 2, late, 0)
+
     def halo_step(kind, ep):
         slot = halo.at[kind, ep]
         return remote(slot, slot, halo_forward.at[ep], halo_sem.at[kind, ep], partner)
@@ -264,11 +269,6 @@
                 step.wait_recv()
                 step.start()
 
-    def late(block, carry):
-        fill_basis(block)
-        return carry
-
-    lax.fori_loop(blocks // 2, blocks, late, 0)
     for dp, de in chips:
         chip, ep = turned(dp, de)
         slot = blk.at[ep, chip * 2 + 1 - core]
@@ -438,6 +438,7 @@
                 {"obj": lax.rem(me_o + k * GROUP, obj_n), "ep": me_e},
             ))
             copies[-1].start()
+        fill_basis(blocks // 2 + 2 * it)
         for k in range(1, planes):
             copies[k - 1].wait()
             packed = packed + part_recv[it, k - 1]
@@ -458,6 +459,7 @@
                 {"obj": q * GROUP + lax.rem(r + dr, GROUP), "ep": lax.rem(me_e + de, ep_n)},
             ))
             copies[-1].start()
+        fill_basis(blocks // 2 + 2 * it + 1)
         for copy in copies:
             copy.wait()
         for ep in range(ep_n):

time: 37.4 us -> 35.8 us (0.957)
  Pallas kernels: 36.6 us -> 35 us
    pallas_call x1, Pallas kernels: 34.3 us -> 33.1 us  [per_device(): pl.pallas_call(functools.partial(detrend_kernel, obj_n, ep_n, order), out...]
where the time goes in v3:
time: 35.8 us; the launch traced here: 35.6 us
  Pallas kernels  35 us (98%)
  between operations  0.64 us (2%)
    pallas_call x1, Pallas kernels, per_device(): pl.pallas_call(functools.partial(detrend_kernel, obj_n, ep_n, order), out...  33.1 us
    pallas_call x1, Pallas kernels, per_device(): pl.pallas_call(spectrum_kernel, out_shape=(jax.ShapeDtypeStruct((rows, co...  1.94 us

profile of v3, /device:TPU:0, one launch (start us, length us, event | category | flops | bytes accessed | tf_op | source)
XLA Modules:
  0.0 35.6 jit_solution(877164757222195301)
XLA Ops:
  0.6 33.1 %shard_map.86 = (f32[128,128]{1,0:T(8,128)S(1)}, bf16[2,64,256]{2,1,0:T(8,128)(2,1)S(1)}, bf16[8,4,256,256]{3,2,1,0:T(8,128)(2,1)S(1)}) custom-call(f32[128,128]{1,0:T(8,128)} %lc_hbm.1, s32[128,128]{1,0:T(8,128)} %valid_hbm.1, s32[1,128]{1,0:T(1,128)} %bitcast.8, f32[1,128]{1,0:T(1,128)} %bitcast.9, f32[16,128]{1,0:T(8,128)} %bitcast.5, f32[1,256]{1,0:T(1,128)} %bitcast.7, ...), custom_call_target="tpu_custom_call" | custom-call | tf_op jit(solution)/shard_map/pallas_call | solution.py:592
  33.7 1.9 %shard_map.87 = (f32[128,128]{1,0:T(8,128)}, f32[64,2048]{1,0:T(8,128)}) custom-call(f32[128,128]{1,0:T(8,128)S(1)} %get-tuple-element.5.left_ref, bf16[2,64,256]{2,1,0:T(8,128)(2,1)S(1)} %get-tuple-element.6.ready_ref, bf16[8,4,256,256]{3,2,1,0:T(8,128)(2,1)S(1)} %get-tuple-element.7.basis_ref), custom_call_target="tpu_custom_call" | custom-call | tf_op jit(solution)/shard_map/pallas_call | solution.py:646

commit v4 on v3

--- a/solution.py
+++ b/solution.py
@@ -30,6 +30,14 @@
 def halves(values):
     high = values.astype(BF16)
     return high, (values - high.astype(F32)).astype(BF16)
+
+
+def left_parts(parts, axis):
+    return jnp.concatenate([parts[0], parts[1], parts[0]], axis=axis)
+
+
+def right_parts(parts, axis):
+    return jnp.concatenate([parts[0], parts[0], parts[1]], axis=axis)
 
 
 def cyclic_outer(vectors):
@@ -80,7 +88,7 @@
     obj_n, ep_n, order, lc_hbm, valid_hbm, pixel_hbm, sigma_hbm, modes_hbm,
     jitter_hbm, freq_hbm, resid_ref, ready_ref, basis_s,
     lc_ref, valid_ref, pixel_ref, sigma_ref, jitter_ref, freq_ref, times_s,
-    blk, halo_send, halo, first, lens, mens, sres, coef_s, modes_s, gram_s, tall_s,
+    blk, halo_send, halo, first, lens, mens, sres, coef_s, modes_s, gram_s, tall_s, square_s,
     part_send, part_recv, solved_s, mode_send, mode_recv, final_s,
     load_sem, near_sem, forward_sem, blk_sem, halo_out, halo_forward, halo_sem, first_sem,
     part_sem, mode_sem,
@@ -269,6 +277,32 @@
                 step.wait_recv()
                 step.start()
 
+    def unpack(t, values, sigma):
+        total = square = jnp.zeros((1, rows), F32)
+        for ep, value in enumerate(values):
+            seen = value < 0.5 * ABSENT
+            scale = jnp.where(seen, sigma, 0.0)
+            at = slice(ep * cols, (ep + 1) * cols)
+            mens[t, at] = scale
+            scaled = value * scale
+            lens[t, at] = scaled
+            sres[t, at] = scaled
+            square = square + jnp.sum(scaled * scaled, axis=0, keepdims=True)
+            total = total + jnp.sum(seen.astype(F32), axis=0, keepdims=True)
+        square_s[t] = square
+        return total
+
+    def unpack_block(side):
+        for dp in range(GROUP // 2):
+            t = lax.rem(p + dp, GROUP // 2) * 2 + side
+            total = unpack(
+                t, [blk[ep, t, :cols] for ep in range(ep_n)], blk[0, t, cols + 1 : cols + 2]
+            )
+            totals.append(total)
+            total_pixels.append(blk[0, t, cols : cols + 1])
+
+    totals, total_pixels = [], []
+    unpack_block(core)
     for dp, de in chips:
         chip, ep = turned(dp, de)
         slot = blk.at[ep, chip * 2 + 1 - core]
@@ -294,39 +328,29 @@
             for ep in range(ep_n):
                 halo_step(kind, ep).wait_send()
 
+    unpack_block(1 - core)
     pixel_level = lax.broadcasted_iota(jnp.int32, (pixels, rows), 0).astype(F32)
     marked = [blk[0, t, cols:] for t in range(GROUP)]
     before, after = halo[0, 0, half:], pltpu.roll(halo[1, 0, half:], rows // 2, 1)
     marked.append(jnp.where(low_half, before, after))
     pixel_row = [m[0:1] for m in marked]
     sigma_row = [m[1:2] for m in marked]
-    totals = []
-    for t in range(tiles):
-        total = jnp.zeros((1, rows), F32)
-        for ep in range(ep_n):
-            if t < GROUP:
-                value = blk[ep, t, :cols]
-            else:
-                prev, follow = halo[0, ep, :half], halo[1, ep, :half]
-                value = jnp.concatenate([
-                    jnp.where(low_half, prev, pltpu.roll(follow, rows // 2, 1)),
-                    jnp.where(low_half, pltpu.roll(prev, rows // 2, 1), follow),
-                ], axis=0)
-            seen = value < 0.5 * ABSENT
-            scale = jnp.where(seen, sigma_row[t], 0.0)
-            at = slice(ep * cols, (ep + 1) * cols)
-            mens[t, at] = scale
-            lens[t, at] = value * scale
-            total = total + jnp.sum(seen.astype(F32), axis=0, keepdims=True)
-        totals.append(total)
-
+    around = []
+    for ep in range(ep_n):
+        prev, follow = halo[0, ep, :half], halo[1, ep, :half]
+        around.append(jnp.concatenate([
+            jnp.where(low_half, prev, pltpu.roll(follow, rows // 2, 1)),
+            jnp.where(low_half, pltpu.roll(prev, rows // 2, 1), follow),
+        ], axis=0))
+    totals.append(unpack(GROUP, around, sigma_row[GROUP]))
+    total_pixels.append(pixel_row[GROUP])
     def by_pixel(tile_rows, tile_pixels):
         gathered = jnp.zeros((pixels, rows), F32)
         for row, where in zip(tile_rows, tile_pixels):
             gathered = gathered + jnp.where(where == pixel_level, row, 0.0)
         return jnp.sum(gathered, axis=1, keepdims=True)
 
-    inverse_count = 1.0 / jnp.maximum(by_pixel(totals, pixel_row), 1.0)
+    inverse_count = 1.0 / jnp.maximum(by_pixel(totals, total_pixels), 1.0)
 
     def limits(squares, tile_pixels, wanted):
         sums = by_pixel(squares, tile_pixels)
@@ -353,76 +377,75 @@
         )
         return jnp.dot(tall_s[...], wide, preferred_element_type=F32)
 
+    runs = [list(range(t, min(t + 2, tiles))) for t in range(0, tiles, 2)]
+
     def scaled_residuals():
         squares = []
-        for t in range(tiles):
-            left = lens[t] - mens[t] * fitted(coef_s[t * order : (t + 1) * order])
-            sres[t] = left
-            squares.append(jnp.sum(left * left, axis=0, keepdims=True))
+        for group in runs:
+            fit = fitted(jnp.concatenate(
+                [coef_s[t * order : (t + 1) * order] for t in group], axis=1
+            ))
+            for n, t in enumerate(group):
+                left = lens[t] - mens[t] * fit[:, n * rows : (n + 1) * rows]
+                sres[t] = left
+                squares.append(jnp.sum(left * left, axis=0, keepdims=True))
         return squares
 
     def reach(left, limit, sigma):
         return (sigma * limit) / jnp.maximum(jnp.abs(left), limit)
 
-    coef_s[...] = jnp.zeros_like(coef_s)
     for ep in range(ep_n):
         modes_s[:, ep * cols : (ep + 1) * cols] = first[ep]
     modes_factor()
 
     def iteration(it, carry):
-        limit = limits(scaled_residuals(), pixel_row, pixel_row)
+        @pl.when(it > 0)
+        def _():
+            for t, square in enumerate(scaled_residuals()):
+                square_s[t] = square
+
+        limit = limits([square_s[t] for t in range(tiles)], pixel_row, pixel_row)
         modes = modes_s[...]
-        outer_high, outer_low = halves(cyclic_outer(modes))
-        modes_high, modes_low = halves(modes)
-        for t in range(tiles):
-            factor = reach(sres[t], limit[t], sigma_row[t])
-            weight, weight_low = halves(mens[t] * factor)
-            value_high, value_low = halves(lens[t] * factor)
-            gram = jnp.dot(outer_high, weight, preferred_element_type=F32)
-            gram = gram + jnp.dot(outer_low, weight, preferred_element_type=F32)
-            gram = gram + jnp.dot(outer_high, weight_low, preferred_element_type=F32)
-            target = jnp.dot(modes_high, value_high, preferred_element_type=F32)
-            target = target + jnp.dot(modes_low, value_high, preferred_element_type=F32)
-            target = target + jnp.dot(modes_high, value_low, preferred_element_type=F32)
-            gram_s[t * depth : t * depth + pairs] = gram
-            gram_s[t * depth + pairs : (t + 1) * depth] = target
+        outers = left_parts(halves(cyclic_outer(modes)), 1)
+        factors = left_parts(halves(modes), 1)
+        for group in runs:
+            weight, value = [], []
+            for t in group:
+                factor = reach(sres[t], limit[t], sigma_row[t])
+                weight.append(right_parts(halves(mens[t] * factor), 0))
+                value.append(right_parts(halves(lens[t] * factor), 0))
+            gram = jnp.dot(outers, jnp.concatenate(weight, axis=1), preferred_element_type=F32)
+            target = jnp.dot(factors, jnp.concatenate(value, axis=1), preferred_element_type=F32)
+            for n, t in enumerate(group):
+                at = slice(n * rows, (n + 1) * rows)
+                gram_s[t * depth : t * depth + pairs] = gram[:, at]
+                gram_s[t * depth + pairs : (t + 1) * depth] = target[:, at]
         solved = damped_solve(lambda row: gram_s[pl.ds(row, tiles, stride=depth), :], order)
         for k in range(order):
             coef_s[pl.ds(k, tiles, stride=order), :] = solved[k]
 
         limit = limits(scaled_residuals(), pixel_row, pixel_row[:GROUP])
         at = pl.ds(pl.multiple_of(me_e * cols + r * slab, slab), slab)
-        weights, weight_lows, value_highs, value_lows, outers, coefs = [], [], [], [], [], []
+        weights, values, outers, coefs = [], [], [], []
         for t in range(GROUP):
             factor = reach(sres[t, at], limit[t], sigma_row[t])
-            weight, weight_low = halves(mens[t, at] * factor)
-            weights.append(weight)
-            weight_lows.append(weight_low)
-            value_high, value_low = halves(lens[t, at] * factor)
-            value_highs.append(value_high)
-            value_lows.append(value_low)
+            weights.append(halves(mens[t, at] * factor))
+            values.append(halves(lens[t, at] * factor))
             coef = coef_s[t * order : (t + 1) * order]
             outers.append(halves(cyclic_outer(coef)))
             coefs.append(halves(coef))
 
-        def copied(parts):
-            return jnp.concatenate([jnp.concatenate(parts, axis=1)] * GROUP, axis=0)
+        def beside(parts):
+            return [jnp.concatenate([pair[n] for pair in parts], axis=1) for n in range(2)]
 
         def across(left, right):
+            copied = jnp.concatenate([right_parts(beside(right), 1)] * GROUP, axis=0)
             return lax.dot_general(
-                left, right, (((1,), (1,)), ((), ())), preferred_element_type=F32
+                left_parts(beside(left), 1), copied, (((1,), (1,)), ((), ())),
+                preferred_element_type=F32,
             )
 
-        weight, weight_low = copied(weights), copied(weight_lows)
-        value_high, value_low = copied(value_highs), copied(value_lows)
-        outer_high = jnp.concatenate([pair[0] for pair in outers], axis=1)
-        outer_low = jnp.concatenate([pair[1] for pair in outers], axis=1)
-        coef_high = jnp.concatenate([pair[0] for pair in coefs], axis=1)
-        coef_low = jnp.concatenate([pair[1] for pair in coefs], axis=1)
-        gram = across(outer_high, weight) + across(outer_low, weight)
-        gram = gram + across(outer_high, weight_low)
-        target = across(coef_high, value_high) + across(coef_low, value_high)
-        target = target + across(coef_high, value_low)
+        gram, target = across(outers, weights), across(coefs, values)
         whole = jnp.concatenate(
             [gram, target, jnp.zeros((GROUP * quarter - depth, rows), F32)], axis=0
         )
@@ -617,6 +640,7 @@
             pltpu.VMEM((order, epochs), F32),
             pltpu.VMEM((tiles * depth, rows), F32),
             pltpu.VMEM((epochs, LANES), BF16),
+            pltpu.VMEM((tiles, 1, rows), F32),
             pltpu.VMEM((ITERS, quarter, rows), F32),
             pltpu.VMEM((ITERS, planes - 1, quarter, rows), F32),
             pltpu.VMEM((order, rows), F32),

time: 35.8 us -> 35.4 us (0.989)
  Pallas kernels: 35 us -> 34.6 us
where the time goes in v4:
time: 35.4 us; the launch traced here: 35.3 us
  Pallas kernels  34.6 us (98%)
  between operations  0.64 us (2%)
    pallas_call x1, Pallas kernels, per_device(): pl.pallas_call(functools.partial(detrend_kernel, obj_n, ep_n, order), out...  32.7 us
    pallas_call x1, Pallas kernels, per_device(): pl.pallas_call(spectrum_kernel, out_shape=(jax.ShapeDtypeStruct((rows, co...  1.95 us

profile of v4, /device:TPU:0, one launch (start us, length us, event | category | flops | bytes accessed | tf_op | source)
XLA Modules:
  0.0 35.3 jit_solution(17475106597268786205)
XLA Ops:
  0.6 32.7 %shard_map.86 = (f32[128,128]{1,0:T(8,128)S(1)}, bf16[2,64,256]{2,1,0:T(8,128)(2,1)S(1)}, bf16[8,4,256,256]{3,2,1,0:T(8,128)(2,1)S(1)}) custom-call(f32[128,128]{1,0:T(8,128)} %lc_hbm.1, s32[128,128]{1,0:T(8,128)} %valid_hbm.1, s32[1,128]{1,0:T(1,128)} %bitcast.8, f32[1,128]{1,0:T(1,128)} %bitcast.9, f32[16,128]{1,0:T(8,128)} %bitcast.5, f32[1,256]{1,0:T(1,128)} %bitcast.7, ...), custom_call_target="tpu_custom_call" | custom-call | tf_op jit(solution)/shard_map/pallas_call | solution.py:615
  33.3 1.9 %shard_map.87 = (f32[128,128]{1,0:T(8,128)}, f32[64,2048]{1,0:T(8,128)}) custom-call(f32[128,128]{1,0:T(8,128)S(1)} %get-tuple-element.5.left_ref, bf16[2,64,256]{2,1,0:T(8,128)(2,1)S(1)} %get-tuple-element.6.ready_ref, bf16[8,4,256,256]{3,2,1,0:T(8,128)(2,1)S(1)} %get-tuple-element.7.basis_ref), custom_call_target="tpu_custom_call" | custom-call | tf_op jit(solution)/shard_map/pallas_call | solution.py:670

commit v5 on v4

--- a/solution.py
+++ b/solution.py
@@ -471,7 +471,9 @@
         solved = damped_solve(lambda row: gram_s[row : row + 1, :], order)
         for k in range(order):
             solved_s[k : k + 1] = solved[k]
-        fresh = pltpu.roll(solved_s[...], r * slab, 1)
+        fresh = jnp.where(
+            lane < slab, solved_s[: order // 2], pltpu.roll(solved_s[order // 2 :], slab, 1)
+        )
         mode_send[it] = fresh
         mode_recv[it, me_e, r] = fresh
         copies = []
@@ -486,10 +488,17 @@
         for copy in copies:
             copy.wait()
         for ep in range(ep_n):
-            joined = mode_recv[it, ep, 0]
-            for k in range(1, GROUP):
-                joined = jnp.where(lane >= k * slab, mode_recv[it, ep, k], joined)
-            modes_s[:, ep * cols : (ep + 1) * cols] = joined
+            sent = [mode_recv[it, ep, k] for k in range(GROUP)]
+            for part in range(2):
+                placed = [
+                    sent[k] if k == part else pltpu.roll(sent[k], (k - part) * slab % rows, 1)
+                    for k in range(GROUP)
+                ]
+                whole = placed[0]
+                for k in range(1, GROUP):
+                    whole = jnp.where(lane >= k * slab, placed[k], whole)
+                at = slice(part * order // 2, (part + 1) * order // 2)
+                modes_s[at, ep * cols : (ep + 1) * cols] = whole
         modes_factor()
         return carry
 
@@ -644,8 +653,8 @@
             pltpu.VMEM((ITERS, quarter, rows), F32),
             pltpu.VMEM((ITERS, planes - 1, quarter, rows), F32),
             pltpu.VMEM((order, rows), F32),
-            pltpu.VMEM((ITERS, order, rows), F32),
-            pltpu.VMEM((ITERS, ep_n, GROUP, order, rows), F32),
+            pltpu.VMEM((ITERS, order // 2, rows), F32),
+            pltpu.VMEM((ITERS, ep_n, GROUP, order // 2, rows), F32),
             pltpu.VMEM((2, rows, epochs), BF16),
             sem((7,)),
             sem((chips,)),

time: 35.4 us -> 35.4 us (level)
  no operation moved by 1% of the time
where the time goes in v5:
time: 35.4 us; the launch traced here: 35.2 us
  Pallas kernels  34.6 us (98%)
  between operations  0.64 us (2%)
    pallas_call x1, Pallas kernels, per_device(): pl.pallas_call(functools.partial(detrend_kernel, obj_n, ep_n, order), out...  32.6 us
    pallas_call x1, Pallas kernels, per_device(): pl.pallas_call(spectrum_kernel, out_shape=(jax.ShapeDtypeStruct((rows, co...  1.95 us

profile of v5, /device:TPU:0, one launch (start us, length us, event | category | flops | bytes accessed | tf_op | source)
XLA Modules:
  0.0 35.2 jit_solution(3369374231756029411)
XLA Ops:
  0.6 32.6 %shard_map.86 = (f32[128,128]{1,0:T(8,128)S(1)}, bf16[2,64,256]{2,1,0:T(8,128)(2,1)S(1)}, bf16[8,4,256,256]{3,2,1,0:T(8,128)(2,1)S(1)}) custom-call(f32[128,128]{1,0:T(8,128)} %lc_hbm.1, s32[128,128]{1,0:T(8,128)} %valid_hbm.1, s32[1,128]{1,0:T(1,128)} %bitcast.8, f32[1,128]{1,0:T(1,128)} %bitcast.9, f32[16,128]{1,0:T(8,128)} %bitcast.5, f32[1,256]{1,0:T(1,128)} %bitcast.7, ...), custom_call_target="tpu_custom_call" | custom-call | tf_op jit(solution)/shard_map/pallas_call | solution.py:624
  33.3 1.9 %shard_map.87 = (f32[128,128]{1,0:T(8,128)}, f32[64,2048]{1,0:T(8,128)}) custom-call(f32[128,128]{1,0:T(8,128)S(1)} %get-tuple-element.5.left_ref, bf16[2,64,256]{2,1,0:T(8,128)(2,1)S(1)} %get-tuple-element.6.ready_ref, bf16[8,4,256,256]{3,2,1,0:T(8,128)(2,1)S(1)} %get-tuple-element.7.basis_ref), custom_call_target="tpu_custom_call" | custom-call | tf_op jit(solution)/shard_map/pallas_call | solution.py:679

commit v6 on v5

--- a/solution.py
+++ b/solution.py
@@ -17,7 +17,7 @@
 HIGHEST = lax.Precision.HIGHEST
 LANES = 128
 SUB = 8
-UNROLL = 4
+UNROLL = 8
 ROOM = 24 << 20
 GROUP = 4
 ABSENT = 1e30
@@ -88,7 +88,7 @@
     obj_n, ep_n, order, lc_hbm, valid_hbm, pixel_hbm, sigma_hbm, modes_hbm,
     jitter_hbm, freq_hbm, resid_ref, ready_ref, basis_s,
     lc_ref, valid_ref, pixel_ref, sigma_ref, jitter_ref, freq_ref, times_s,
-    blk, halo_send, halo, first, lens, mens, sres, coef_s, modes_s, gram_s, tall_s, square_s,
+    blk, halo_send, halo, first, lens, mens, sres, coef_s, modes_s, gram_s, tall_s, square_s, wide_s,
     part_send, part_recv, solved_s, mode_send, mode_recv, final_s,
     load_sem, near_sem, forward_sem, blk_sem, halo_out, halo_forward, halo_sem, first_sem,
     part_sem, mode_sem,
@@ -162,7 +162,7 @@
     )
 
     def fill_basis(block):
-        begin = pl.multiple_of(block * width, width)
+        begin = block * width if isinstance(block, int) else pl.multiple_of(block * width, width)
         freqs = (freq_ref[:, pl.ds(begin, width)] + 1).astype(F32) / (4.0 * epochs)
 
         def strip(step, carry):
@@ -301,6 +301,21 @@
             totals.append(total)
             total_pixels.append(blk[0, t, cols : cols + 1])
 
+    def modes_factor():
+        high, low = halves(modes_s[...])
+        stacked = jnp.concatenate([high, high, low], axis=0).astype(F32)
+        stacked = jnp.concatenate(
+            [stacked, jnp.zeros((LANES - 3 * order, epochs), F32)], axis=0
+        )
+        tall_s[...] = stacked.T.astype(BF16)
+
+    for de in range(1, ep_n):
+        ep = lax.rem(me_e + de, ep_n)
+        remote(first.at[ep], first.at[ep], first_sem.at[0, de], first_sem.at[1, ep], partner).wait_recv()
+    wide_s[...] = jnp.zeros_like(wide_s)
+    for ep in range(ep_n):
+        modes_s[:, ep * cols : (ep + 1) * cols] = first[ep]
+    modes_factor()
     totals, total_pixels = [], []
     unpack_block(core)
     for dp, de in chips:
@@ -312,9 +327,6 @@
         def _():
             for ep in range(ep_n):
                 halo_step(kind, ep).wait_recv()
-    for de in range(1, ep_n):
-        ep = lax.rem(me_e + de, ep_n)
-        remote(first.at[ep], first.at[ep], first_sem.at[0, de], first_sem.at[1, ep], partner).wait_recv()
     for copy in near + forwards + greetings:
         copy.wait_send()
     for kind, there, sends, _, _ in halo_kinds:
@@ -362,19 +374,12 @@
             for where in wanted
         ]
 
-    def modes_factor():
-        high, low = halves(modes_s[...])
-        stacked = jnp.concatenate([high, high, low], axis=0).astype(F32)
-        stacked = jnp.concatenate(
-            [stacked, jnp.zeros((LANES - 3 * order, epochs), F32)], axis=0
-        )
-        tall_s[...] = stacked.T.astype(BF16)
-
-    def fitted(coef):
-        high, low = halves(coef)
-        wide = jnp.concatenate(
-            [high, low, high, jnp.zeros((LANES - 3 * order, coef.shape[1]), BF16)], axis=0
-        )
+    def widen():
+        for t in range(tiles):
+            high, low = halves(coef_s[t * order : (t + 1) * order])
+            wide_s[t, : 3 * order] = jnp.concatenate([high, low, high], axis=0)
+
+    def fitted(wide):
         return jnp.dot(tall_s[...], wide, preferred_element_type=F32)
 
     runs = [list(range(t, min(t + 2, tiles))) for t in range(0, tiles, 2)]
@@ -382,9 +387,7 @@
     def scaled_residuals():
         squares = []
         for group in runs:
-            fit = fitted(jnp.concatenate(
-                [coef_s[t * order : (t + 1) * order] for t in group], axis=1
-            ))
+            fit = fitted(jnp.concatenate([wide_s[t] for t in group], axis=1))
             for n, t in enumerate(group):
                 left = lens[t] - mens[t] * fit[:, n * rows : (n + 1) * rows]
                 sres[t] = left
@@ -394,13 +397,9 @@
     def reach(left, limit, sigma):
         return (sigma * limit) / jnp.maximum(jnp.abs(left), limit)
 
-    for ep in range(ep_n):
-        modes_s[:, ep * cols : (ep + 1) * cols] = first[ep]
-    modes_factor()
 
     def iteration(it, carry):
-        @pl.when(it > 0)
-        def _():
+        if it > 0:
             for t, square in enumerate(scaled_residuals()):
                 square_s[t] = square
 
@@ -423,6 +422,7 @@
         solved = damped_solve(lambda row: gram_s[pl.ds(row, tiles, stride=depth), :], order)
         for k in range(order):
             coef_s[pl.ds(k, tiles, stride=order), :] = solved[k]
+        widen()
 
         limit = limits(scaled_residuals(), pixel_row, pixel_row[:GROUP])
         at = pl.ds(pl.multiple_of(me_e * cols + r * slab, slab), slab)
@@ -502,16 +502,16 @@
         modes_factor()
         return carry
 
-    lax.fori_loop(0, ITERS, iteration, 0)
+    for it in range(ITERS):
+        iteration(it, 0)
     own_coef = coef_s[pl.ds(pl.multiple_of(r * order, order), order), :]
     beside = jnp.where(
         me_e < ep_n // 2, jnp.where(r == 0, GROUP, r - 1), r + 1
     )
-    side_coef = coef_s[pl.ds(pl.multiple_of(beside * order, order), order), :]
     both_pixels, squares = [], []
     lefts = []
-    for t, coef in ((r, own_coef), (beside, side_coef)):
-        left = lens[t] - mens[t] * fitted(coef)
+    for t in (r, beside):
+        left = lens[t] - mens[t] * fitted(wide_s[t])
         lefts.append(left)
         squares.append(jnp.sum(left * left, axis=0, keepdims=True))
     for t, name in ((r, 0), (beside, 1)):
@@ -650,6 +650,7 @@
             pltpu.VMEM((tiles * depth, rows), F32),
             pltpu.VMEM((epochs, LANES), BF16),
             pltpu.VMEM((tiles, 1, rows), F32),
+            pltpu.VMEM((tiles, LANES, rows), BF16),
             pltpu.VMEM((ITERS, quarter, rows), F32),
             pltpu.VMEM((ITERS, planes - 1, quarter, rows), F32),
             pltpu.VMEM((order, rows), F32),

time: 35.4 us -> 34.9 us (0.986)
  Pallas kernels: 34.6 us -> 34.1 us
where the time goes in v6:
time: 34.9 us; the launch traced here: 34.8 us
  Pallas kernels  34.1 us (98%)
  between operations  0.64 us (2%)
    pallas_call x1, Pallas kernels, per_device(): pl.pallas_call(functools.partial(detrend_kernel, obj_n, ep_n, order), out...  32.5 us
    pallas_call x1, Pallas kernels, per_device(): pl.pallas_call(spectrum_kernel, out_shape=(jax.ShapeDtypeStruct((rows, co...  1.69 us

profile of v6, /device:TPU:0, one launch (start us, length us, event | category | flops | bytes accessed | tf_op | source)
XLA Modules:
  0.0 34.8 jit_solution(9270995124566499863)
XLA Ops:
  0.6 32.5 %shard_map.86 = (f32[128,128]{1,0:T(8,128)S(1)}, bf16[2,64,256]{2,1,0:T(8,128)(2,1)S(1)}, bf16[8,4,256,256]{3,2,1,0:T(8,128)(2,1)S(1)}) custom-call(f32[128,128]{1,0:T(8,128)} %lc_hbm.1, s32[128,128]{1,0:T(8,128)} %valid_hbm.1, s32[1,128]{1,0:T(1,128)} %bitcast.8, f32[1,128]{1,0:T(1,128)} %bitcast.9, f32[16,128]{1,0:T(8,128)} %bitcast.5, f32[1,256]{1,0:T(1,128)} %bitcast.7, ...), custom_call_target="tpu_custom_call" | custom-call | tf_op jit(solution)/shard_map/pallas_call | solution.py:624
  33.1 1.7 %shard_map.87 = (f32[128,128]{1,0:T(8,128)}, f32[64,2048]{1,0:T(8,128)}) custom-call(f32[128,128]{1,0:T(8,128)S(1)} %get-tuple-element.5.left_ref, bf16[2,64,256]{2,1,0:T(8,128)(2,1)S(1)} %get-tuple-element.6.ready_ref, bf16[8,4,256,256]{3,2,1,0:T(8,128)(2,1)S(1)} %get-tuple-element.7.basis_ref), custom_call_target="tpu_custom_call" | custom-call | tf_op jit(solution)/shard_map/pallas_call | solution.py:680

commit v7 on v6

--- a/solution.py
+++ b/solution.py
@@ -327,19 +327,6 @@
         def _():
             for ep in range(ep_n):
                 halo_step(kind, ep).wait_recv()
-    for copy in near + forwards + greetings:
-        copy.wait_send()
-    for kind, there, sends, _, _ in halo_kinds:
-        @pl.when(sends)
-        def _():
-            for copy in halo_copies(kind, there):
-                copy.wait_send()
-    for kind, _, _, arrives, passes in halo_kinds:
-        @pl.when(jnp.logical_and(arrives, passes))
-        def _():
-            for ep in range(ep_n):
-                halo_step(kind, ep).wait_send()
-
     unpack_block(1 - core)
     pixel_level = lax.broadcasted_iota(jnp.int32, (pixels, rows), 0).astype(F32)
     marked = [blk[0, t, cols:] for t in range(GROUP)]
@@ -463,8 +450,9 @@
             copies[-1].start()
         fill_basis(blocks // 2 + 2 * it)
         for k in range(1, planes):
-            copies[k - 1].wait()
+            copies[k - 1].wait_recv()
             packed = packed + part_recv[it, k - 1]
+        sent.extend(copies)
         gram_s[:quarter] = packed
         for k in range(1, GROUP):
             gram_s[k * quarter : (k + 1) * quarter] = pltpu.roll(packed, rows - k * slab, 1)
@@ -485,13 +473,14 @@
             ))
             copies[-1].start()
         fill_basis(blocks // 2 + 2 * it + 1)
+        sent.extend(copies)
         for copy in copies:
-            copy.wait()
+            copy.wait_recv()
         for ep in range(ep_n):
-            sent = [mode_recv[it, ep, k] for k in range(GROUP)]
+            heard = [mode_recv[it, ep, k] for k in range(GROUP)]
             for part in range(2):
                 placed = [
-                    sent[k] if k == part else pltpu.roll(sent[k], (k - part) * slab % rows, 1)
+                    heard[k] if k == part else pltpu.roll(heard[k], (k - part) * slab % rows, 1)
                     for k in range(GROUP)
                 ]
                 whole = placed[0]
@@ -502,6 +491,7 @@
         modes_factor()
         return carry
 
+    sent = []
     for it in range(ITERS):
         iteration(it, 0)
     own_coef = coef_s[pl.ds(pl.multiple_of(r * order, order), order), :]
@@ -531,6 +521,20 @@
     )
     mine_at = pl.ds(pl.multiple_of(me_e * share, share), share)
     ready_ref[...] = final_s[:, mine_at, :]
+    for copy in sent:
+        copy.wait_send()
+    for copy in near + forwards + greetings:
+        copy.wait_send()
+    for kind, there, sends, _, _ in halo_kinds:
+        @pl.when(sends)
+        def _():
+            for copy in halo_copies(kind, there):
+                copy.wait_send()
+    for kind, _, _, arrives, passes in halo_kinds:
+        @pl.when(jnp.logical_and(arrives, passes))
+        def _():
+            for ep in range(ep_n):
+                halo_step(kind, ep).wait_send()
 
 
 def spectrum_kernel(left_ref, ready_ref, basis_ref, resid_hbm, power_hbm, power_s, sems):

time: 34.9 us -> 34.4 us (0.986)
  Pallas kernels: 34.1 us -> 33.6 us
    pallas_call x1, Pallas kernels: 32.5 us -> 31.9 us  [per_device(): pl.pallas_call(functools.partial(detrend_kernel, obj_n, ep_n, order), out...]
where the time goes in v7:
time: 34.4 us; the launch traced here: 34.3 us
  Pallas kernels  33.6 us (98%)
  between operations  0.64 us (2%)
    pallas_call x1, Pallas kernels, per_device(): pl.pallas_call(functools.partial(detrend_kernel, obj_n, ep_n, order), out...  31.9 us
    pallas_call x1, Pallas kernels, per_device(): pl.pallas_call(spectrum_kernel, out_shape=(jax.ShapeDtypeStruct((rows, co...  1.69 us

profile of v7, /device:TPU:0, one launch (start us, length us, event | category | flops | bytes accessed | tf_op | source)
XLA Modules:
  0.0 34.3 jit_solution(5930967937664027451)
XLA Ops:
  0.6 31.9 %shard_map.86 = (f32[128,128]{1,0:T(8,128)S(1)}, bf16[2,64,256]{2,1,0:T(8,128)(2,1)S(1)}, bf16[8,4,256,256]{3,2,1,0:T(8,128)(2,1)S(1)}) custom-call(f32[128,128]{1,0:T(8,128)} %lc_hbm.1, s32[128,128]{1,0:T(8,128)} %valid_hbm.1, s32[1,128]{1,0:T(1,128)} %bitcast.8, f32[1,128]{1,0:T(1,128)} %bitcast.9, f32[16,128]{1,0:T(8,128)} %bitcast.5, f32[1,256]{1,0:T(1,128)} %bitcast.7, ...), custom_call_target="tpu_custom_call" | custom-call | tf_op jit(solution)/shard_map/pallas_call | solution.py:628
  32.6 1.7 %shard_map.87 = (f32[128,128]{1,0:T(8,128)}, f32[64,2048]{1,0:T(8,128)}) custom-call(f32[128,128]{1,0:T(8,128)S(1)} %get-tuple-element.5.left_ref, bf16[2,64,256]{2,1,0:T(8,128)(2,1)S(1)} %get-tuple-element.6.ready_ref, bf16[8,4,256,256]{3,2,1,0:T(8,128)(2,1)S(1)} %get-tuple-element.7.basis_ref), custom_call_target="tpu_custom_call" | custom-call | tf_op jit(solution)/shard_map/pallas_call | solution.py:684
